TPU v7x, 32 devices: a whole 2x2x4 slice. The times are simulated.
32 devices in a mesh: row: 4 (over y, x), col: 8 (over z, core).
Axes of the slice: x: 2, y: 2, z: 4, core: 2. Of those that a mesh axis runs over, the one named last changes fastest.
Arguments:
- trail: float32 [2, 4, 512, 2, 8, 512], P(None, 'row', None, None, 'col'), may hold values from -6 to 6
- panel: float32 [2, 4, 512, 512], P(None, 'row', None, 'col'), may hold values from -6 to 6
- row_basis: float32 [2, 4, 64, 512], P(None, 'row', None, 'col'), may hold values from -0.75 to 0.75
- row_coeff: float32 [2, 4, 64, 512], P(None, 'row', None, 'col'), may hold values from -0.25 to 0.25
- col_basis: float32 [2, 8, 64, 512], P(None, 'col', None, 'row'), may hold values from -0.75 to 0.75
- col_scaled: float32 [2, 8, 64, 512], P(None, 'col', None, 'row'), may hold values from -0.25 to 0.25
- pivot_basis: float32 [64, 512], P(None, 'col'), may hold values from -0.75 to 0.75
- pivot_scaled: float32 [64, 512], replicated, may hold values from -0.25 to 0.25
- sketch: float32 [64, 512], replicated, may hold values from -6 to 6
- perm: int32 [512], replicated, may hold values from 0 to 511, each once
- pair_kind: int32 [256], replicated, may hold values from 0 to 1
- pivot_values: float32 [3, 256], replicated, may hold values from -3 to 3, as said below
Outputs:
- trail_out: float32 [2, 4, 512, 2, 8, 512], P(None, 'row', None, None, 'col')
- basis_out: float32 [2, 4, 64, 512], P(None, 'row')
- coeff_out: float32 [2, 4, 64, 512], P(None, 'row')
Inputs may be any that keep to these rules, and one draw needn't show every extreme that they name: `pivot_values`: rows 0 and 1 have magnitudes between 0.5 and 0.7; row 2 has magnitude 1.2 or more.
All inputs are finite; a program needn't handle non-finite values.
Results may differ from a plain program's by a relative error of at most 0.00013.
Values sent between devices are 32-bit elements; how exact they have to be, the bound alone decides.
No kernel may reach another device: no remote copies, remote signals or barrier semaphores. Data moves between devices by JAX's collectives and lax.ppermute only.
A program may use at most 64 MiB of HBM per device.

v0:
```python
import jax
import jax.numpy as jnp
from jax import lax
from jax.sharding import PartitionSpec as P


def pair_apply(rows, pair_kind, pivot_values):
    shaped = rows.reshape(rows.shape[:-1] + (rows.shape[-1] // 2, 2))
    first_in = shaped[..., 0]
    second_in = shaped[..., 1]
    diag_one = pivot_values[0]
    diag_two = pivot_values[1]
    offdiag = pivot_values[2]
    determinant = diag_one * diag_two - offdiag * offdiag
    twin = pair_kind == 1
    first = jnp.where(
        twin, (first_in * diag_two - second_in * offdiag) / determinant, first_in / diag_one
    )
    second = jnp.where(
        twin, (second_in * diag_one - first_in * offdiag) / determinant, second_in / diag_two
    )
    return jnp.stack([first, second], axis=-1).reshape(rows.shape)


def tri_solve(lower, rhs):
    return jax.vmap(lambda low, right: jax.scipy.linalg.solve_triangular(low, right, lower=True))(
        lower, rhs
    )


def body(
    trail,
    panel,
    row_basis,
    row_coeff,
    col_basis,
    col_scaled,
    pivot_basis,
    pivot_scaled,
    sketch,
    perm,
    pair_kind,
    pivot_values,
):
    highest = lax.Precision.HIGHEST
    width = sketch.shape[1]
    block = panel.shape[3]
    xrows, yrows = (
        lax.all_gather(row_basis, "col", axis=3, tiled=True),
        lax.all_gather(row_coeff, "col", axis=3, tiled=True),
    )
    zcols, gcols = (
        lax.all_gather(col_basis, "row", axis=3, tiled=True),
        lax.all_gather(col_scaled, "row", axis=3, tiled=True),
    )
    xrows = xrows[:, 0]
    yrows = yrows[:, 0]
    zcols = zcols[:, 0]
    gcols = gcols[:, 0]
    core = jnp.einsum("arp,bsp->arbs", yrows, gcols, precision=highest)
    left = jnp.einsum("arp,arbs->apbs", xrows, core, precision=highest)
    change = jnp.einsum("apbs,bsq->apbq", left, zcols, precision=highest)
    trail_out = trail - change[:, None, :, :, None, :]
    pcore = jnp.einsum("arp,sp->ars", yrows, pivot_scaled, precision=highest)
    pleft = jnp.einsum("arp,ars->aps", xrows, pcore, precision=highest)
    updated = panel[:, 0] - jnp.einsum("aps,sq->apq", pleft, pivot_basis, precision=highest)
    scaled_t = pair_apply(sketch, pair_kind, pivot_values)
    column_ids = lax.axis_index("col") * block + jnp.arange(block, dtype=jnp.int32)
    selector = (perm[:, None] == column_ids[None, :]).astype(jnp.float32)
    local_sketch = jnp.dot(scaled_t, selector, precision=highest)
    partial_range = jnp.einsum("apq,rq->arp", updated, local_sketch, precision=highest)
    range_t = lax.psum(partial_range, "col")
    gram = jnp.einsum("arp,asp->ars", range_t, range_t, precision=highest) / width
    basis = tri_solve(jnp.linalg.cholesky(gram), range_t)
    projected_part = jnp.einsum("arp,apq->arq", basis, updated, precision=highest)
    projected = lax.all_gather(projected_part, "col", axis=2, tiled=True)
    permuted = jnp.take(projected, perm, axis=2)
    coeff = pair_apply(permuted, pair_kind, pivot_values) / jnp.sqrt(jnp.float32(width))
    return (trail_out, basis[:, None], coeff[:, None])


def solution(mesh):
    return jax.shard_map(
        body,
        mesh=mesh,
        in_specs=(
            P(None, "row", None, None, "col", None),
            P(None, "row", None, "col"),
            P(None, "row", None, "col"),
            P(None, "row", None, "col"),
            P(None, "col", None, "row"),
            P(None, "col", None, "row"),
            P(None, "col"),
            P(),
            P(),
            P(),
            P(),
            P(),
        ),
        out_specs=(
            P(None, "row", None, None, "col", None),
            P(None, "row", None, None),
            P(None, "row", None, None),
        ),
        check_vma=False,
    )
```

profile of v0, /device:TPU:0, one launch (start us, length us, event | category | flops | bytes accessed | tf_op | source)
XLA Modules:
  0.0 159.1 jit_solution(12313392400558865005)
XLA Ops:
  7.3 0.8 broadcast_compare_fusion
  8.1 0.8 fusion.16
  8.9 0.9 copy.54
  9.8 0.9 copy.51
  10.8 1.0 copy.59
  11.8 16.5 %all_gather.15 = f32[2,1,64,512]{2,0,1,3:T(2,128)S(1)} all-gather(f32[2,1,64,64]{2,0,1,3:T(2,128)S(1)} %copy.51), channel_id=1, replica_groups=mesh['row'=4,'col'=8] {'col'}, dimensions={3}, use_global_device_ids=true | all-gather | bytes 294912 | tf_op jit(solution)/shard_map/all_gather | solution.py:50
  28.5 14.8 %all_gather.17 = f32[2,1,64,512]{2,0,1,3:T(2,128)S(1)} all-gather(f32[2,1,64,64]{2,0,1,3:T(2,128)S(1)} %copy.54), channel_id=1, replica_groups=mesh['row'=4,'col'=8] {'col'}, dimensions={3}, use_global_device_ids=true | all-gather | bytes 294912 | tf_op jit(solution)/shard_map/all_gather | solution.py:49
  43.5 2.2 %broadcast_select_fusion.4 = (f32[64,256,1]{0,2,1:T(1,128)S(1)}, f32[64,256,1]{0,2,1:T(1,128)S(1)}) fusion(pred[256]{0:T(512)(128)(4,1)S(1)} %broadcast_compare_fusion, f32[64,256,2]{0,2,1:T(2,128)S(1)} %bitcast.82, f32[256]{0:T(256)S(1)} %bitcast.90, f32[256]{0:T(256)S(1)} %bitcast.96, f32[256]{0:T(256)S(1)} %bitcast.93, f32[256]{0:T(256)S(1)} %bitcast.87), kind=kLoop, calls=%fused_computation.21 | loop fusion | flops 196608 | bytes 266496 | tf_op jit(solution)/shard_map/jit(_where)/select_n | solution.py:16
  47.7 1.1 convolution_bitcast_fusion.1
  48.9 10.3 %all_gather.18 = f32[2,1,64,512]{3,2,0,1:T(8,128)S(1)} all-gather(f32[2,1,64,128]{3,2,0,1:T(8,128)S(1)} %bitcast.85), channel_id=1, replica_groups=mesh['row'=4,'col'=8] {'row'}, dimensions={3}, use_global_device_ids=true | all-gather | bytes 327680 | tf_op jit(solution)/shard_map/all_gather | solution.py:53
  59.2 10.2 %all_gather.16 = f32[2,1,64,512]{3,2,0,1:T(8,128)S(1)} all-gather(f32[2,1,64,128]{3,2,0,1:T(8,128)S(1)} %bitcast.86), channel_id=1, replica_groups=mesh['row'=4,'col'=8] {'row'}, dimensions={3}, use_global_device_ids=true | all-gather | bytes 327680 | tf_op jit(solution)/shard_map/all_gather | solution.py:54
  69.9 0.6 convolution_bitcast_fusion
  70.5 7.2 %bitcast_subtract_fusion = f32[2,1,512,2,1,512]{5,2,0,3,4,1:T(8,128)} fusion(f32[2,1,512,2,1,512]{5,4,3,2,1,0:T(1,128)} %param.12, f32[2,512,2,64]{1,3,0,2:T(8,128)S(1)} %convolution_bitcast_fusion, f32[2,1,64,512]{3,2,0,1:T(8,128)S(1)} %all_gather.18), kind=kOutput, calls=%fused_computation.1 | convolution fusion | flops 806354944 | bytes 9175040 | tf_op jit(solution)/shard_map/apbs,bsq->apbq/dot_general | solution.py:62
  77.9 8.5 %copy.66 = f32[2,1,512,2,1,512]{5,4,3,2,1,0:T(1,128)} copy(f32[2,1,512,2,1,512]{5,2,0,3,4,1:T(8,128)} %bitcast_subtract_fusion) | data formatting | bytes 8388608
  86.4 19.4 %all-reduce.2.cloned.1.call-done = f32[2,64,512]{2,1,0:T(8,128)} async-done(((f32[2,64,512]{2,1,0:T(8,128)}), f32[2,64,512]{2,1,0:T(8,128)}) %all-reduce.2.cloned.1.call-update) | async-done | bytes 262160 | tf_op jit(solution)/shard_map/psum | solution.py:72
  105.8 1.4 fusion.17
  107.3 11.7 %custom-call.8 = f32[2,64,64]{2,1,0:T(8,128)S(1)} custom-call(f32[2,64,64]{2,1,0:T(8,128)S(1)} %fusion.14), custom_call_target="Cholesky" | custom-call | tf_op jit(solution)/shard_map/jit(cholesky)/cholesky | solution.py:74
  119.3 9.8 %custom-call.9 = f32[2,1,64,64]{2,3,1,0:T(8,128)S(1)} custom-call(f32[2,1,64,64]{3,2,1,0:T(8,128)S(1)} %select_bitcast_fusion), custom_call_target="InvertDiagBlocksLowerTriangular" | custom-call | tf_op jit(solution)/shard_map/vmap(jit(_solve_triangular))/triangular_solve | solution.py:26
  129.1 1.4 fusion.12
  131.0 15.1 %all_gather.19 = f32[2,64,512]{1,0,2:T(2,128)S(1)} all-gather(f32[2,64,64]{1,0,2:T(2,128)S(1)} %copy.64), channel_id=1, replica_groups=mesh['row'=4,'col'=8] {'col'}, dimensions={2}, use_global_device_ids=true | all-gather | bytes 294912 | tf_op jit(solution)/shard_map/all_gather | solution.py:76
  146.1 2.1 %gather_fusion = f32[512,2,64]{2,1,0:T(2,128)S(1)} fusion(f32[2,64,512]{1,0,2:T(2,128)S(1)} %all_gather.19, s32[1024]{0:T(1024)S(1)} %pad_clamp_fusion), kind=kCustom, calls=%fused_computation | custom fusion | bytes 526336 | tf_op jit(solution)/shard_map/jit(_take)/gather | solution.py:77
  148.6 2.2 %broadcast_select_fusion.1 = (f32[2,64,256,1]{1,3,2,0:T(1,128)S(1)}, f32[2,64,256,1]{1,3,2,0:T(1,128)S(1)}) fusion(pred[256]{0:T(512)(128)(4,1)S(1)} %broadcast_compare_fusion, f32[2,64,256,2]{1,3,2,0:T(2,128)S(1)} %broadcast_select_fusion.2, f32[256]{0:T(256)S(1)} %bitcast.92, f32[256]{0:T(256)S(1)} %multiply_subtract_fusion, f32[256]{0:T(256)S(1)} %bitcast.95, ...), kind=kLoop, calls=%fused_computation.9 | loop fusion | flops 393216 | bytes 528640 | tf_op jit(solution)/shard_map/jit(_where)/select_n | solution.py:16
  150.8 0.6 maximum_multiply_fusion
  151.4 0.9 copy.68
  (41 shorter events, 4.4 us)
Async XLA Ops:
  7.2 38.8 %copy-start = (f32[64,512]{1,0:T(8,128)S(1)}, f32[64,512]{1,0:T(8,128)}, u32[]{:S(2)}) copy-start(f32[64,512]{1,0:T(8,128)} %param.19) | copy-start | bytes 393220
  7.2 39.7 %copy-start.6 = (s32[512]{0:T(512)S(1)}, s32[512]{0:T(512)}, u32[]{:S(2)}) copy-start(s32[512]{0:T(512)} %param.21) | copy-start | bytes 6148
  7.2 40.1 %copy-start.5 = (f32[64,64]{1,0:T(8,128)S(1)}, f32[64,64]{1,0:T(8,128)}, u32[]{:S(2)}) copy-start(f32[64,64]{1,0:T(8,128)} %param.18) | copy-start | bytes 49156
  7.2 40.1 %copy-start.2 = (f32[2,1,512,64]{2,3,1,0:T(8,128)S(1)}, f32[2,1,512,64]{2,3,1,0:T(8,128)}, u32[]{:S(2)}) copy-start(f32[2,1,512,64]{2,3,1,0:T(8,128)} %param.13) | copy-start | bytes 786436
  7.2 41.7 %copy-start.3 = (f32[2,1,64,128]{3,2,1,0:T(8,128)S(1)}, f32[2,1,64,128]{3,2,1,0:T(8,128)}, u32[]{:S(2)}) copy-start(f32[2,1,64,128]{3,2,1,0:T(8,128)} %param.16) | copy-start | bytes 196612
  7.2 52.0 %copy-start.4 = (f32[2,1,64,128]{3,2,1,0:T(8,128)S(1)}, f32[2,1,64,128]{3,2,1,0:T(8,128)}, u32[]{:S(2)}) copy-start(f32[2,1,64,128]{3,2,1,0:T(8,128)} %param.17) | copy-start | bytes 196612
  7.2 98.6 %all-reduce.2.cloned.1.call-start = ((), (), s32[]{:S(2)}) async-start(), calls=%async_computation | async-start | bytes 524288 | tf_op jit(solution)/shard_map/psum | solution.py:72
  130.5 21.8 %copy-start.1 = (f32[2,64,512]{2,1,0:T(8,128)}, f32[2,64,512]{2,1,0:T(8,128)S(1)}, u32[]{:S(2)}) copy-start(f32[2,64,512]{2,1,0:T(8,128)S(1)} %fusion.12) | copy-start | bytes 786436
Sparse Core Ops, SparseCore 0:
  49.0 56.7 all-reduce.1
where the time goes:
time: 160 us; the launch traced here: 159 us
  blocking collectives  66.8 us (42%)
  other arithmetic  29.1 us (18%)
  waiting for transfers between devices  19.4 us (12%)
  local copies, waits for them, and re-layouts  15.2 us (10%)
  between operations  14.4 us (9%)
  matrix products  14.3 us (9%)
    psum x1, waiting for transfers between devices, body(): range_t = lax.psum(partial_range, 'col')  19.4 us
    all_gather x1, blocking collectives, body(): lax.all_gather(row_coeff, 'col', axis=3, tiled=True)  16.5 us
    all_gather x1, blocking collectives, body(): projected = lax.all_gather(projected_part, 'col', axis=2, tiled=True)  15.1 us
    all_gather x1, blocking collectives, body(): lax.all_gather(row_basis, 'col', axis=3, tiled=True)  14.8 us
    unnamed x19, local copies, waits for them, and re-layouts  12.3 us
    another operation x4, other arithmetic, body(): basis = tri_solve(jnp.linalg.cholesky(gram), range_t)  11.9 us
    all_gather x1, blocking collectives, body(): lax.all_gather(col_basis, 'row', axis=3, tiled=True)  10.3 us
    all_gather x1, blocking collectives, body(): lax.all_gather(col_scaled, 'row', axis=3, tiled=True)  10.2 us
  transfers between devices with their start and end apart: 1, of which 1 were waited for; matrix products, arithmetic and copies ran while one was open for 11% of the time, Pallas kernels for 0%

commit v1 on v0

--- a/solution.py
+++ b/solution.py
@@ -51,7 +51,7 @@
     )
     zcols, gcols = (
         lax.all_gather(col_basis, "row", axis=3, tiled=True),
-        lax.all_gather(col_scaled, "row", axis=3, tiled=True),
+        jnp.concatenate(lax.all_gather(col_scaled, "row"), 3),
     )
     xrows = xrows[:, 0]
     yrows = yrows[:, 0]

time: 160 us -> 160 us (level)
  no operation moved by 1% of the time
where the time goes in v1:
time: 160 us; the launch traced here: 159 us
  blocking collectives  66.1 us (41%)
  other arithmetic  29.1 us (18%)
  waiting for transfers between devices  19.8 us (12%)
  local copies, waits for them, and re-layouts  15.4 us (10%)
  between operations  14.4 us (9%)
  matrix products  14.2 us (9%)
    psum x1, waiting for transfers between devices, body(): range_t = lax.psum(partial_range, 'col')  19.8 us
    all_gather x1, blocking collectives, body(): lax.all_gather(row_coeff, 'col', axis=3, tiled=True)  16.5 us
    all_gather x1, blocking collectives, body(): projected = lax.all_gather(projected_part, 'col', axis=2, tiled=True)  15.1 us
    all_gather x1, blocking collectives, body(): lax.all_gather(row_basis, 'col', axis=3, tiled=True)  14.8 us
    unnamed x19, local copies, waits for them, and re-layouts  12.3 us
    another operation x4, other arithmetic, body(): basis = tri_solve(jnp.linalg.cholesky(gram), range_t)  11.9 us
    all_gather x1, blocking collectives, body(): lax.all_gather(col_basis, 'row', axis=3, tiled=True)  10.3 us
    another operation x3, other arithmetic, tri_solve(): jax.scipy.linalg.solve_triangular(low, right, lower=True)  9.92 us
  transfers between devices with their start and end apart: 1, of which 1 were waited for; matrix products, arithmetic and copies ran while one was open for 11% of the time, Pallas kernels for 0%

profile of v1, /device:TPU:0, one launch (start us, length us, event | category | flops | bytes accessed | tf_op | source)
XLA Modules:
  0.0 159.1 jit_solution(5318945160354107534)
XLA Ops:
  7.3 0.8 broadcast_compare_fusion
  8.1 0.8 fusion.16
  8.9 0.9 copy.55
  9.8 0.9 copy.52
  10.8 1.0 copy.60
  11.8 16.5 %all_gather.18 = f32[2,1,64,512]{2,0,1,3:T(2,128)S(1)} all-gather(f32[2,1,64,64]{2,0,1,3:T(2,128)S(1)} %copy.52), channel_id=1, replica_groups=mesh['row'=4,'col'=8] {'col'}, dimensions={3}, use_global_device_ids=true | all-gather | bytes 294912 | tf_op jit(solution)/shard_map/all_gather | solution.py:50
  28.5 14.8 %all_gather.21 = f32[2,1,64,512]{2,0,1,3:T(2,128)S(1)} all-gather(f32[2,1,64,64]{2,0,1,3:T(2,128)S(1)} %copy.55), channel_id=1, replica_groups=mesh['row'=4,'col'=8] {'col'}, dimensions={3}, use_global_device_ids=true | all-gather | bytes 294912 | tf_op jit(solution)/shard_map/all_gather | solution.py:49
  43.5 2.2 %broadcast_select_fusion.4 = (f32[64,256,1]{0,2,1:T(1,128)S(1)}, f32[64,256,1]{0,2,1:T(1,128)S(1)}) fusion(pred[256]{0:T(512)(128)(4,1)S(1)} %broadcast_compare_fusion, f32[64,256,2]{0,2,1:T(2,128)S(1)} %bitcast.84, f32[256]{0:T(256)S(1)} %bitcast.93, f32[256]{0:T(256)S(1)} %bitcast.99, f32[256]{0:T(256)S(1)} %bitcast.96, f32[256]{0:T(256)S(1)} %bitcast.90), kind=kLoop, calls=%fused_computation.22 | loop fusion | flops 196608 | bytes 266496 | tf_op jit(solution)/shard_map/jit(_where)/select_n | solution.py:16
  47.7 1.1 convolution_bitcast_fusion.1
  48.9 10.3 %all_gather.22 = f32[2,1,64,512]{3,2,0,1:T(8,128)S(1)} all-gather(f32[2,1,64,128]{3,2,0,1:T(8,128)S(1)} %bitcast.89), channel_id=1, replica_groups=mesh['row'=4,'col'=8] {'row'}, dimensions={3}, use_global_device_ids=true | all-gather | bytes 327680 | tf_op jit(solution)/shard_map/all_gather | solution.py:53
  59.2 9.5 %all-gather = f32[8,1,64,128]{3,2,1,0:T(8,128)S(1)} all-gather(f32[2,1,64,128]{3,2,1,0:T(8,128)S(1)} %copy-done.4), channel_id=2, replica_groups=mesh['row'=4,'col'=8] {'row'}, dimensions={0}, use_global_device_ids=true | all-gather | bytes 327680 | tf_op jit(solution)/shard_map/all_gather | solution.py:54
  69.5 0.6 convolution_bitcast_fusion
  70.1 7.2 %bitcast_subtract_fusion = f32[2,1,512,2,1,512]{5,2,0,3,4,1:T(8,128)} fusion(f32[2,1,512,2,1,512]{5,4,3,2,1,0:T(1,128)} %param.12, f32[2,512,2,64]{1,3,0,2:T(8,128)S(1)} %convolution_bitcast_fusion, f32[2,1,64,512]{3,2,0,1:T(8,128)S(1)} %all_gather.22), kind=kOutput, calls=%fused_computation.1 | convolution fusion | flops 806354944 | bytes 9175040 | tf_op jit(solution)/shard_map/apbs,bsq->apbq/dot_general | solution.py:62
  77.5 8.5 %copy.67 = f32[2,1,512,2,1,512]{5,4,3,2,1,0:T(1,128)} copy(f32[2,1,512,2,1,512]{5,2,0,3,4,1:T(8,128)} %bitcast_subtract_fusion) | data formatting | bytes 8388608
  86.0 19.8 %all-reduce.2.cloned.1.call-done = f32[2,64,512]{2,1,0:T(8,128)} async-done(((f32[2,64,512]{2,1,0:T(8,128)}), f32[2,64,512]{2,1,0:T(8,128)}) %all-reduce.2.cloned.1.call-update) | async-done | bytes 262160 | tf_op jit(solution)/shard_map/psum | solution.py:72
  105.8 1.4 fusion.17
  107.3 11.7 %custom-call.8 = f32[2,64,64]{2,1,0:T(8,128)S(1)} custom-call(f32[2,64,64]{2,1,0:T(8,128)S(1)} %fusion.14), custom_call_target="Cholesky" | custom-call | tf_op jit(solution)/shard_map/jit(cholesky)/cholesky | solution.py:74
  119.3 9.8 %custom-call.9 = f32[2,1,64,64]{2,3,1,0:T(8,128)S(1)} custom-call(f32[2,1,64,64]{3,2,1,0:T(8,128)S(1)} %select_bitcast_fusion), custom_call_target="InvertDiagBlocksLowerTriangular" | custom-call | tf_op jit(solution)/shard_map/vmap(jit(_solve_triangular))/triangular_solve | solution.py:26
  129.1 1.4 fusion.12
  131.0 15.1 %all_gather.23 = f32[2,64,512]{1,0,2:T(2,128)S(1)} all-gather(f32[2,64,64]{1,0,2:T(2,128)S(1)} %copy.65), channel_id=1, replica_groups=mesh['row'=4,'col'=8] {'col'}, dimensions={2}, use_global_device_ids=true | all-gather | bytes 294912 | tf_op jit(solution)/shard_map/all_gather | solution.py:76
  146.1 2.1 %gather_fusion = f32[512,2,64]{2,1,0:T(2,128)S(1)} fusion(f32[2,64,512]{1,0,2:T(2,128)S(1)} %all_gather.23, s32[1024]{0:T(1024)S(1)} %pad_clamp_fusion), kind=kCustom, calls=%fused_computation | custom fusion | bytes 526336 | tf_op jit(solution)/shard_map/jit(_take)/gather | solution.py:77
  148.6 2.2 %broadcast_select_fusion.1 = (f32[2,64,256,1]{1,3,2,0:T(1,128)S(1)}, f32[2,64,256,1]{1,3,2,0:T(1,128)S(1)}) fusion(pred[256]{0:T(512)(128)(4,1)S(1)} %broadcast_compare_fusion, f32[2,64,256,2]{1,3,2,0:T(2,128)S(1)} %broadcast_select_fusion.2, f32[256]{0:T(256)S(1)} %bitcast.95, f32[256]{0:T(256)S(1)} %multiply_subtract_fusion, f32[256]{0:T(256)S(1)} %bitcast.98, ...), kind=kLoop, calls=%fused_computation.9 | loop fusion | flops 393216 | bytes 528640 | tf_op jit(solution)/shard_map/jit(_where)/select_n | solution.py:16
  150.8 0.6 maximum_multiply_fusion
  151.4 0.9 copy.69
  (43 shorter events, 4.7 us)
Async XLA Ops:
  7.2 38.8 %copy-start = (f32[64,512]{1,0:T(8,128)S(1)}, f32[64,512]{1,0:T(8,128)}, u32[]{:S(2)}) copy-start(f32[64,512]{1,0:T(8,128)} %param.19) | copy-start | bytes 393220
  7.2 39.7 %copy-start.6 = (s32[512]{0:T(512)S(1)}, s32[512]{0:T(512)}, u32[]{:S(2)}) copy-start(s32[512]{0:T(512)} %param.21) | copy-start | bytes 6148
  7.2 40.1 %copy-start.5 = (f32[64,64]{1,0:T(8,128)S(1)}, f32[64,64]{1,0:T(8,128)}, u32[]{:S(2)}) copy-start(f32[64,64]{1,0:T(8,128)} %param.18) | copy-start | bytes 49156
  7.2 40.1 %copy-start.2 = (f32[2,1,512,64]{2,3,1,0:T(8,128)S(1)}, f32[2,1,512,64]{2,3,1,0:T(8,128)}, u32[]{:S(2)}) copy-start(f32[2,1,512,64]{2,3,1,0:T(8,128)} %param.13) | copy-start | bytes 786436
  7.2 41.7 %copy-start.3 = (f32[2,1,64,128]{3,2,1,0:T(8,128)S(1)}, f32[2,1,64,128]{3,2,1,0:T(8,128)}, u32[]{:S(2)}) copy-start(f32[2,1,64,128]{3,2,1,0:T(8,128)} %param.16) | copy-start | bytes 196612
  7.2 52.0 %copy-start.4 = (f32[2,1,64,128]{3,2,1,0:T(8,128)S(1)}, f32[2,1,64,128]{3,2,1,0:T(8,128)}, u32[]{:S(2)}) copy-start(f32[2,1,64,128]{3,2,1,0:T(8,128)} %param.17) | copy-start | bytes 196612
  7.2 98.6 %all-reduce.2.cloned.1.call-start = ((), (), s32[]{:S(2)}) async-start(), calls=%async_computation | async-start | bytes 524288 | tf_op jit(solution)/shard_map/psum | solution.py:72
  130.5 21.8 %copy-start.1 = (f32[2,64,512]{2,1,0:T(8,128)}, f32[2,64,512]{2,1,0:T(8,128)S(1)}, u32[]{:S(2)}) copy-start(f32[2,64,512]{2,1,0:T(8,128)S(1)} %fusion.12) | copy-start | bytes 786436
Sparse Core Ops, SparseCore 0:
  49.0 56.7 all-reduce.1
